TPU v7x, 32 devices: a whole 2x2x4 slice. The times are simulated.
32 devices in a mesh: dp: 8 (over y, x, core), tensor: 4 (over z).
Axes of the slice: x: 2, y: 2, z: 4, core: 2. Of those that a mesh axis runs over, the one named last changes fastest.
Arguments:
- tokens: bfloat16 [2, 8192, 1024], P(None, ('dp', 'tensor')), may hold values from -6 to 6
- attn_gain: float32 [1024], replicated, may hold values from 0.25 to 1.75
- ffn_gain: float32 [1024], replicated, may hold values from 0.25 to 1.75
- query_weight: bfloat16 [1024, 1024], P(None, 'tensor'), may hold values from -0.1875 to 0.1875
- key_weight: bfloat16 [1024, 1024], P(None, 'tensor'), may hold values from -0.1875 to 0.1875
- value_weight: bfloat16 [1024, 1024], P(None, 'tensor'), may hold values from -0.1875 to 0.1875
- out_weight: bfloat16 [1024, 1024], P('tensor'), may hold values from -1 to 1
- gate_weight: bfloat16 [1024, 2816], P(None, 'tensor'), may hold values from -0.1875 to 0.1875
- up_weight: bfloat16 [1024, 2816], P(None, 'tensor'), may hold values from -0.1875 to 0.1875
- down_weight: bfloat16 [2816, 1024], P('tensor'), may hold values from -0.109375 to 0.109375
- cache_keys: bfloat16 [2, 2048, 1024], P(None, 'dp', 'tensor'), may hold values from -6 to 6
- cache_values: bfloat16 [2, 2048, 1024], P(None, 'dp', 'tensor'), may hold values from -6 to 6
- knn_index: int32 [2, 32, 8, 128], P(None, 'dp', 'tensor'), may hold values from 0 to 511, all different within a row
- cotangent: bfloat16 [2, 8192, 1024], P(None, ('dp', 'tensor')), may hold values from -6 to 6
Outputs:
- output: bfloat16 [2, 8192, 1024], P(None, ('dp', 'tensor'))
- grad_tokens: bfloat16 [2, 8192, 1024], P(None, ('dp', 'tensor'))
- grad_query: float32 [1024, 1024], P(None, 'tensor')
- grad_key: float32 [1024, 1024], P(None, 'tensor')
- grad_value: float32 [1024, 1024], P(None, 'tensor')
- grad_outproj: float32 [1024, 1024], P('tensor')
- grad_gate: float32 [1024, 2816], P(None, 'tensor')
- grad_up: float32 [1024, 2816], P(None, 'tensor')
- grad_down: float32 [2816, 1024], P('tensor')
- grad_attn_gain: float32 [1024], replicated
- grad_ffn_gain: float32 [1024], replicated
Inputs may be any that keep to these rules, and one draw needn't show every extreme that they name: knn_index[m, s * 4 + b, h] lists 128 distinct candidate rows read in head h by the queries of block b of sequence s of micro-batch m; an entry e < 256 is row e of the sequence's own cache, an entry e >= 256 is row e - 256 of the cache of sequence s - 1 of the same micro-batch, sequence 0 taking sequence 8 - 1.
All inputs are finite; a program needn't handle non-finite values.
Results may differ from a plain program's by a relative error of at most 0.02.
Values may be sent and summed in bfloat16 or wider, within the bound.
A program may use at most 192 MiB of HBM per device.

v0:
```python
import functools

import jax
import jax.numpy as jnp
from jax import lax
from jax.experimental import pallas as pl
from jax.experimental.pallas import tpu as pltpu
from jax.sharding import Mesh
from jax.sharding import PartitionSpec as P

HEADS = 8
HD = 128
MICRO = 2
BLK = 256
TOPK = 128
CACHE = 256
D = 1024
NQ = 4
DP = D // NQ
HALF = 512
LEN = 1024
HID = 352
RA = 4 * HD
RB = 3 * HID

EPS = 1e-06
NEG = -1e30
BF = jnp.bfloat16
F32 = jnp.float32


def nn(a, b):
    return lax.dot_general(a, b, (((1,), (0,)), ((), ())), preferred_element_type=F32)


def nt(a, b):
    return lax.dot_general(a, b, (((1,), (1,)), ((), ())), preferred_element_type=F32)


def tn(a, b):
    return lax.dot_general(a, b, (((0,), (0,)), ((), ())), preferred_element_type=F32)


VM = pl.BlockSpec(memory_space=pltpu.VMEM)


def call(body, outs, args, flops=0, trans=0, scratch=(), name=None, vmem=None):
    nbytes = sum(a.size * a.dtype.itemsize for a in args) + sum(
        jnp.dtype(t).itemsize * functools.reduce(lambda x, y: x * y, s, 1) for s, t in outs
    )
    return pl.pallas_call(
        body,
        out_shape=[jax.ShapeDtypeStruct(s, t) for s, t in outs],
        in_specs=[VM for _ in args],
        out_specs=[VM for _ in outs],
        scratch_shapes=list(scratch),
        name=name,
        compiler_params=pltpu.CompilerParams(vmem_limit_bytes=vmem),
        cost_estimate=pl.CostEstimate(flops=int(flops), bytes_accessed=int(nbytes), transcendentals=int(trans)),
    )(*args)


def block(index, size):
    return pl.ds(pl.multiple_of(index * size, size), size)


def lanes(k):
    return slice(k * DP, (k + 1) * DP)


def scale_of(x):
    return lax.rsqrt(jnp.mean(x * x, axis=-1, keepdims=True) + EPS)


def norm_back(grad, x, gain):
    scale = scale_of(x)
    scaled = grad * gain
    gain_part = jnp.sum(grad * x * scale, axis=0, keepdims=True)
    back = scale * scaled - x * (scale * scale * scale) * jnp.mean(scaled * x, axis=-1, keepdims=True)
    return back, gain_part


def causal():
    return lax.broadcasted_iota(jnp.int32, (BLK, BLK), 1) <= lax.broadcasted_iota(jnp.int32, (BLK, BLK), 0)


def place_a_body(got, gq, gk, gv, go):
    for half in range(2):
        rows = slice(half * HD, (half + 1) * HD)
        for i, out in enumerate((gq, gk, gv)):
            out[:, rows] = got[half, i * HD : (i + 1) * HD, :].astype(F32).T
        go[rows, :] = got[half, 3 * HD : 4 * HD, :].astype(F32)


def place_b_body(got, *outs):
    for half in range(2):
        for i, out in enumerate(outs):
            out[half * HID : (half + 1) * HID, :] = got[half, i * HID : (i + 1) * HID, :].astype(F32)


def where_am_i():
    return lax.axis_index("r"), lax.axis_index("q"), lax.axis_index("c"), lax.axis_index("t")


def at(q, c, t):
    return {"q": q, "c": c, "t": t}


def dp_at(index):
    return {"r": index // (2 * NQ), "q": lax.rem(index // 2, NQ), "c": lax.rem(index, 2)}


def remote(src, dst, send_sem, recv_sem, device):
    return pltpu.make_async_remote_copy(
        src_ref=src, dst_ref=dst, send_sem=send_sem, recv_sem=recv_sem, device_id=device,
        device_id_type=pl.DeviceIdType.MESH,
    )


def arrived(dst, recv_sem, spare):
    pltpu.make_async_copy(dst, dst, recv_sem).wait()


def greet(devices):
    barrier = pltpu.get_barrier_semaphore()
    for device in devices:
        pl.semaphore_signal(barrier, inc=1, device_id=device, device_id_type=pl.DeviceIdType.MESH)
    pl.semaphore_wait(barrier, len(devices))


class Sends:
    def __init__(self):
        self.open = []

    def go(self, src, dst, send_sem, recv_sem, device, when=None):
        copy = remote(src, dst, send_sem, recv_sem, device)
        self.open.append((copy, when))
        if when is None:
            copy.start()
        else:
            pl.when(when)(copy.start)

    def drain(self):
        for copy, when in self.open:
            if when is None:
                copy.wait_send()
            else:
                pl.when(when)(copy.wait_send)
        self.open = []


def front_body(tok, cot, gain_a, gain_f, ck, cv, knn, wq, wk, wv, wo, gate_t, up_t, down,
               wa, wb, x_own, n_own, n_oth, cot_own, cot_oth, mem, qkv, att, lse, hidden, n2_own, n2_oth,
               prev_k, prev_v, picked, o_send, o_got,
               row_send, row_recv, cot_send, cot_recv, cache_send, cache_recv, mem_send, mem_recv,
               za_send, za_recv, xa_send, xa_recv, zb_send, zb_recv, xb_send, xb_recv, pair_send, pair_recv):
    r, q, c, t = where_am_i()
    count = lax.axis_size("r") * 2 * NQ
    me = (r * NQ + q) * 2 + c
    after = dp_at(lax.rem(me + 1, count))
    across = dp_at(lax.rem(me + jnp.where(c == 0, count - 1, 1), count))
    mid = (t == 1) | (t == 2)
    second, third = jnp.where(mid, 3, 2), jnp.where(mid, 2, 3)
    partner = at(q, 1 - c, t)
    sends = Sends()
    greet(
        [at(q, c, t ^ j) for j in range(1, 4)] + [at(q, 1 - c, t ^ j) for j in range(4)]
        + [at(q ^ 1, c, t), at(q ^ 2, c, t), at(q ^ 3, c, t), across]
    )

    def rows_out(src, dst, send_sem, recv_sem):
        slot = t & 1
        for m in range(MICRO):
            here = (c == (t >> 1)) & (m == slot)
            for k in range(NQ):
                one = src.at[m, :, block(q ^ k, DP)]
                two = dst.at[block(slot, 256), lanes(k)]
                sends.go(one, two, send_sem.at[m, k], recv_sem.at[slot, k], at(q, t >> 1, 2 * c + m),
                         when=jnp.logical_not(here))
                pl.when(here)(pltpu.make_async_copy(one, two, recv_sem.at[slot, k]).start)

    def rows_in(dst, recv_sem):
        for slot in range(2):
            for k in range(NQ):
                arrived(dst.at[slot * 256 : (slot + 1) * 256, lanes(k)], recv_sem.at[slot, k], None)

    near, far_mid = at(q, c, t ^ 1), at(q, c, t ^ 3)
    ends = jnp.logical_not(mid)
    a_piece = [wa.at[0, :, lanes(0)]]
    b_piece = [w.at[pl.ds(pl.multiple_of(c * HID, 32), HID), block(q, DP)] for w in (gate_t, up_t, down)]

    def a_slot(s):
        return [wa.at[s, :, lanes(0)]]

    def b_slot(s):
        return [wb.at[s - 1, i * HID : (i + 1) * HID, lanes(0)] for i in range(3)]

    def z_first(piece, slot, send_sem, recv_sem):
        for i, (one, two) in enumerate(zip(piece, slot(1))):
            sends.go(one, two, send_sem.at[0, i], recv_sem.at[1, i], near)
        for i, (one, two) in enumerate(zip(piece, slot(3))):
            sends.go(one, two, send_sem.at[1, i], recv_sem.at[3, i], far_mid, when=mid)

    def relay_some(order, s, when, slot, whole, z_send, z_recv, x_send, x_recv):
        for i, two in enumerate(slot(s)):
            if when is None:
                arrived(two, z_recv.at[s, i], None)
            else:
                pl.when(when)(functools.partial(arrived, two, z_recv.at[s, i], None))
        if order == 1:
            for i, (one, two) in enumerate(zip(slot(1), slot(2))):
                sends.go(one, two, z_send.at[2, i], z_recv.at[2, i], far_mid, when=mid)
        elif when is mid:
            back = 2 if order == 2 else 3
            for i, (one, two) in enumerate(zip(slot(s), slot(back))):
                sends.go(one, two, z_send.at[order + 1, i], z_recv.at[back, i], near, when=mid)
        for k in (1, 2, 3) if order == 3 else (1, 2):
            sends.go(whole(s, 0), whole(s, k), x_send.at[s, k], x_recv.at[s, k], at(q ^ k, c, t), when=when)

    def relay_far(order, whole, x_send, x_recv):
        s = (None, 1, second)[order]
        arrived(whole(s, order), x_recv.at[s, order], None)
        sends.go(whole(s, order), whole(s, 3), x_send.at[s, 3], x_recv.at[s, 3], at(q ^ (3 - order), c, t))

    def in_place(order, whole, x_recv):
        s = (None, 1, second, third)[order]
        for k in range(1, NQ):
            if k != order or order == 3:
                arrived(whole(s, k), x_recv.at[s, k], None)

    def a_whole(s, k):
        return wa.at[s, :, lanes(k)]

    def b_whole(s, k):
        return wb.at[s - 1, :, lanes(k)]

    relay_a = functools.partial(relay_some, slot=a_slot, whole=a_whole, z_send=za_send, z_recv=za_recv, x_send=xa_send, x_recv=xa_recv)
    relay_b = functools.partial(relay_some, slot=b_slot, whole=b_whole, z_send=zb_send, z_recv=zb_recv, x_send=xb_send, x_recv=xb_recv)

    for i, (one, two) in enumerate(((ck, prev_k), (cv, prev_v))):
        sends.go(one, two, cache_send.at[i], cache_recv.at[i], after)
    for k in range(NQ):
        rows = block(q ^ k, DP)
        for i, w in enumerate((wq, wk, wv)):
            wa[0, i * HD : (i + 1) * HD, lanes(k)] = w[rows, block(c, HD)].T
        wa[0, 3 * HD : 4 * HD, lanes(k)] = wo[block(c, HD), rows]
        if k == 1:
            z_first(a_piece, a_slot, za_send, za_recv)
            z_first(b_piece, b_slot, zb_send, zb_recv)
            rows_out(tok, x_own, row_send, row_recv)

    relay_a(1, 1, None)
    relay_a(2, 3, mid)
    for i, two in enumerate((prev_k, prev_v)):
        arrived(two, cache_recv.at[i], None)

    def pick(i, carry):
        m, h, b = i // 8, (i // 4) % 2, i % 4
        cols = block(h, HD)
        picks = knn[m, b, pl.ds(h, 1), :]
        rows = lax.broadcasted_iota(jnp.int32, (CACHE, TOPK), 0)
        hot_own = jnp.where(rows == picks, 1.0, 0.0).astype(BF)
        hot_prev = jnp.where(rows + CACHE == picks, 1.0, 0.0).astype(BF)
        for kv, own, prev in ((0, ck, prev_k), (1, cv, prev_v)):
            got = tn(hot_own, own[m, :, cols]) + tn(hot_prev, prev[m, :, cols])
            picked[m, h, pl.ds(pl.multiple_of(kv * 512 + b * TOPK, TOPK), TOPK), :] = got.astype(BF)
        return carry

    lax.fori_loop(0, 16, pick, 0)
    relay_b(1, 1, None)
    relay_b(2, 3, mid)
    relay_far(1, a_whole, xa_send, xa_recv)

    def send_mem():
        for m in range(MICRO):
            for h in range(2):
                kind = t ^ (2 * c + m)
                here = (c == h) & (kind == 0)
                sends.go(picked.at[m, h], mem.at[kind], mem_send.at[m, h], mem_recv.at[kind], at(q, h, 2 * c + m),
                         when=jnp.logical_not(here))
                pl.when(here)(pltpu.make_async_copy(picked.at[m, h], mem.at[kind], mem_recv.at[kind]).start)

    relay_far(1, b_whole, xb_send, xb_recv)
    rows_in(x_own, row_recv)
    gain = jnp.concatenate([gain_a[:, block(q ^ k, DP)] for k in range(NQ)], axis=1)
    for i in range(2):
        rows = slice(i * 256, (i + 1) * 256)
        x = x_own[rows, :].astype(F32)
        n_own[rows, :] = (x * scale_of(x) * gain).astype(BF)
    sends.go(n_own, n_oth, pair_send.at[0], pair_recv.at[0], partner)

    def project(j, who, n):
        acc = nt(n[...], wa[j, 0 : 3 * HD, :])
        rows = block(who, HALF)
        qkv[j, rows, 0:HD] = (acc[:, 0:HD] * (HD**-0.5)).astype(BF)
        qkv[j, rows, HD : 3 * HD] = acc[:, HD : 3 * HD].astype(BF)

    def attend(j):
        keep = causal()
        for b in range(LEN // BLK):
            rows = slice(b * BLK, (b + 1) * BLK)
            query = qkv[j, rows, 0:HD]
            diag = jnp.where(keep, nt(query, qkv[j, rows, HD : 2 * HD]), NEG)
            far = nt(query, mem[j, b * TOPK : (b + 1) * TOPK, :])
            top = jnp.maximum(jnp.max(diag, axis=1, keepdims=True), jnp.max(far, axis=1, keepdims=True))
            if b:
                past = nt(query, qkv[j, 0 : b * BLK, HD : 2 * HD])
                top = jnp.maximum(top, jnp.max(past, axis=1, keepdims=True))
            diag = jnp.exp(diag - top)
            far = jnp.exp(far - top)
            total = jnp.sum(diag, axis=1, keepdims=True) + jnp.sum(far, axis=1, keepdims=True)
            if b:
                past = jnp.exp(past - top)
                total = total + jnp.sum(past, axis=1, keepdims=True)
            inverse = 1.0 / total
            out = nn((diag * inverse).astype(BF), qkv[j, rows, 2 * HD : 3 * HD])
            out = out + nn((far * inverse).astype(BF), mem[j, 512 + b * TOPK : 512 + (b + 1) * TOPK, :])
            if b:
                out = out + nn((past * inverse).astype(BF), qkv[j, 0 : b * BLK, 2 * HD : 3 * HD])
            att[rows, block(j, HD)] = out.astype(BF)
            lse[j, rows, :] = jnp.broadcast_to(top + jnp.log(total), (BLK, HD))

    def got_mem(j):
        arrived(mem.at[j], mem_recv.at[j], None)

    project(0, c, n_own)
    arrived(n_oth, pair_recv.at[0], None)
    project(0, 1 - c, n_oth)
    relay_a(2, 2, ends)
    relay_a(3, 2, mid)
    relay_b(2, 2, ends)
    relay_b(3, 2, mid)
    send_mem()
    rows_out(cot, cot_own, cot_send, cot_recv)
    relay_far(2, a_whole, xa_send, xa_recv)
    in_place(1, a_whole, xa_recv)
    project(1, c, n_own)
    project(1, 1 - c, n_oth)
    got_mem(0)
    attend(0)
    relay_far(2, b_whole, xb_send, xb_recv)
    relay_a(3, 3, ends)
    relay_b(3, 3, ends)
    in_place(2, a_whole, xa_recv)
    project(second, c, n_own)
    project(second, 1 - c, n_oth)
    got_mem(1)
    attend(1)
    in_place(3, a_whole, xa_recv)
    project(third, c, n_own)
    project(third, 1 - c, n_oth)
    got_mem(second)
    attend(second)
    got_mem(third)
    attend(third)

    weights = jnp.concatenate([wa[j, 3 * HD : 4 * HD, :] for j in range(4)], axis=0)
    o_send[...] = nn(att[block(1 - c, HALF), :], weights).astype(BF)
    sends.go(o_send, o_got, pair_send.at[1], pair_recv.at[1], partner)
    hidden[...] = nn(att[block(c, HALF), :], weights)
    rows_in(cot_own, cot_recv)
    sends.go(cot_own, cot_oth, pair_send.at[2], pair_recv.at[2], partner)
    arrived(o_got, pair_recv.at[1], None)
    gain = jnp.concatenate([gain_f[:, block(q ^ k, DP)] for k in range(NQ)], axis=1)
    for i in range(2):
        rows = slice(i * 256, (i + 1) * 256)
        h = x_own[rows, :].astype(F32) + (hidden[rows, :] + o_got[rows, :].astype(F32))
        hidden[rows, :] = h
        n2_own[rows, :] = (h * scale_of(h) * gain).astype(BF)
    sends.go(n2_own, n2_oth, pair_send.at[3], pair_recv.at[3], partner)
    for order in range(1, 4):
        in_place(order, b_whole, xb_recv)
    arrived(n2_oth, pair_recv.at[3], None)
    arrived(cot_oth, pair_recv.at[2], None)
    sends.drain()


def front(*args):
    hbm = pl.BlockSpec(memory_space=pl.ANY)
    outs = [
        ((4, RA, D), BF, VM), ((3, RB, D), BF, hbm), ((HALF, D), BF, VM), ((HALF, D), BF, VM), ((HALF, D), BF, VM),
        ((HALF, D), BF, hbm), ((HALF, D), BF, hbm), ((4, 1024, HD), BF, VM), ((4, LEN, 3 * HD), BF, VM),
        ((LEN, 4 * HD), BF, VM), ((4, LEN, HD), F32, VM), ((HALF, D), F32, VM), ((HALF, D), BF, VM), ((HALF, D), BF, VM),
    ]
    dma = pltpu.SemaphoreType.DMA
    return pl.pallas_call(
        front_body,
        out_shape=[jax.ShapeDtypeStruct(s, d) for s, d, _ in outs],
        in_specs=[hbm, hbm] + [VM] * 9 + [hbm] * 3,
        out_specs=[m for _, _, m in outs],
        scratch_shapes=[
            pltpu.VMEM((MICRO, CACHE, 256), BF), pltpu.VMEM((MICRO, CACHE, 256), BF),
            pltpu.VMEM((MICRO, 2, 1024, HD), BF), pltpu.VMEM((HALF, D), BF), pltpu.VMEM((HALF, D), BF),
            dma((2, 4)), dma((2, 4)), dma((2, 4)), dma((2, 4)), dma((2,)), dma((2,)), dma((2, 2)), dma((4,)),
            dma((5, 1)), dma((4, 1)), dma((4, 4)), dma((4, 4)), dma((5, 3)), dma((4, 3)), dma((4, 4)), dma((4, 4)),
            dma((4,)), dma((4,)),
        ],
        compiler_params=pltpu.CompilerParams(collective_id=0, has_side_effects=True, vmem_limit_bytes=60 << 20),
        name="front",
        cost_estimate=pl.CostEstimate(flops=int(2e10), bytes_accessed=int(5e7), transcendentals=0),
    )(*args)


def everyone(q, c, t):
    return (
        [at(q, c, t ^ j) for j in range(1, 4)] + [at(q, 1 - c, t ^ j) for j in range(4)]
        + [at(q ^ 1, c, t), at(q ^ 2, c, t)]
    )


def add_low(a, b):
    return (a.astype(F32) + b.astype(F32)).astype(BF)


def turn(i):
    return jnp.where(i < 2, 2 * i + 1, 6 - 2 * i)


def slot_of(p, k):
    return (0, (2, 1)[p], (1, 2)[p], 3)[k]


class Plane:
    def __init__(self, chunk, recv1, recv2, sems):
        self.chunk, self.recv1, self.recv2 = chunk, recv1, recv2
        self.s1, self.r1, self.s2, self.r2 = sems
        _, self.q, self.c, self.t = where_am_i()

    def copy1(self, j, p):
        return remote(self.chunk.at[j, p, pl.ds(2, 2)], self.recv1.at[j, p], self.s1.at[j, p], self.r1.at[j, p],
                      at(self.q ^ (1 + p), self.c, self.t))

    def copy2(self, j, p):
        return remote(self.chunk.at[j, p, 1], self.recv2.at[j, p], self.s2.at[j, p], self.r2.at[j, p],
                      at(self.q ^ (2 - p), self.c, self.t))

    def start(self, j):
        for p in range(2):
            self.copy1(j, p).start()

    def stage2(self, j):
        for p in range(2):
            arrived(self.recv1.at[j, p], self.r1.at[j, p], None)
            self.chunk[j, p, 1] = add_low(self.chunk[j, p, 1], self.recv1[j, p, 1])
        self.chunk[j, 0, 0] = add_low(self.chunk[j, 0, 0], self.recv1[j, 0, 0])
        for p in range(2):
            self.copy2(j, p).start()
        self.chunk[j, 1, 0] = add_low(self.chunk[j, 1, 0], self.recv1[j, 1, 0])

    def stage3(self, j, out):
        half = self.chunk.shape[3]
        for p in range(2):
            arrived(self.recv2.at[j, p], self.r2.at[j, p], None)
            out[p * half : (p + 1) * half, :] = add_low(self.chunk[j, p, 0], self.recv2[j, p])

    def drain(self):
        for j in range(4):
            for p in range(2):
                self.copy1(j, p).wait_send()
                self.copy2(j, p).wait_send()


def rows_back(sends, src, dst, send_sem, recv_sem, slots=(0, 1)):
    _, q, c, t = where_am_i()
    m = t & 1
    for s in slots:
        here = (c == (t >> 1)) & (s == m)
        for k in range(NQ):
            one = src.at[s * 256 : (s + 1) * 256, lanes(k)]
            two = dst.at[m, :, block(q ^ k, DP)]
            sends.go(one, two, send_sem.at[s, k], recv_sem.at[m, k], at(q, t >> 1, 2 * c + s),
                     when=jnp.logical_not(here))
            pl.when(here)(pltpu.make_async_copy(one, two, recv_sem.at[m, k]).start)


def rows_back_in(dst, recv_sem):
    _, q, _, _ = where_am_i()
    for m in range(2):
        for k in range(NQ):
            arrived(dst.at[m, :, block(q ^ k, DP)], recv_sem.at[m, k], None)


def put_gain(out, row, total):
    _, q, _, _ = where_am_i()
    for k in range(NQ):
        out[row : row + 1, block(q ^ k, DP)] = total[:, lanes(k)]


def local_gain(gain):
    _, q, _, _ = where_am_i()
    return jnp.concatenate([gain[:, block(q ^ k, DP)] for k in range(NQ)], axis=1)


DMA = pltpu.SemaphoreType.DMA
HBM = pl.BlockSpec(memory_space=pl.ANY)


def remote_call(body, name, number, args, places, outs, scratch, flops):
    return pl.pallas_call(
        body,
        out_shape=[jax.ShapeDtypeStruct(s, d) for s, d, _ in outs],
        in_specs=list(places),
        out_specs=[m for _, _, m in outs],
        scratch_shapes=list(scratch),
        compiler_params=pltpu.CompilerParams(collective_id=number, has_side_effects=True, vmem_limit_bytes=62 << 20),
        name=name,
        cost_estimate=pl.CostEstimate(flops=int(flops), bytes_accessed=int(5e7), transcendentals=0),
    )(*args)


def middle_body(n_own, n_oth, cot_own, cot_oth, hidden, gain_f, gate_t, up_t, down, wb,
                sums, grad_hidden, low_own, low_oth, out_rows, gain_two,
                wgu, wd, act, dgu, chunk, recv1, recv2, z_out, z_in, d_send, d_got, y_send, y_got, rows_buf,
                own_sem, got_sem, s1, r1, s2, r2, z_send, z_recv, pair_send, pair_recv, row_send, row_recv):
    _, q, c, t = where_am_i()
    partner = at(q, 1 - c, t)
    sends = Sends()

    def own_copies():
        rows = pl.ds(pl.multiple_of(c * HID, 32), HID)
        for k in range(NQ):
            for i, (w, two) in enumerate(((gate_t, wgu.at[0:HID, lanes(k)]), (up_t, wgu.at[HID : 2 * HID, lanes(k)]),
                                          (down, wd.at[0:HID, lanes(k)]))):
                yield pltpu.make_async_copy(w.at[rows, block(q ^ k, DP)], two, own_sem.at[i, k])

    def got_copies(j):
        gu = wgu.at[pl.ds(pl.multiple_of(j * (2 * HID), 32), 2 * HID)]
        d = wd.at[pl.ds(pl.multiple_of(j * HID, 32), HID)]
        yield pltpu.make_async_copy(wb.at[j - 1, pl.ds(0, 2 * HID)], gu, got_sem.at[j - 1, 0])
        yield pltpu.make_async_copy(wb.at[j - 1, pl.ds(2 * HID, HID)], d, got_sem.at[j - 1, 1])

    for j in range(1, 4):
        for copy in got_copies(j):
            copy.start()
    for copy in own_copies():
        copy.start()
    greet(everyone(q, c, t))
    plane = Plane(chunk, recv1, recv2, (s1, r1, s2, r2))

    def feed(i, carry):
        j = turn(i)

        @pl.when(j > 0)
        def _():
            for copy in got_copies(j):
                copy.wait()

        @pl.when(j == 0)
        def _():
            for copy in own_copies():
                copy.wait()

        gate_rows = pl.ds(pl.multiple_of(j * (2 * HID), 32), HID)
        up_rows = pl.ds(pl.multiple_of(j * (2 * HID) + HID, 32), HID)
        down_rows = pl.ds(pl.multiple_of(j * HID, 32), HID)
        for side, n, cot in ((0, n_own, cot_own), (1, n_oth, cot_oth)):
            for b in range(2):
                rows = slice(b * 256, (b + 1) * 256)
                cols = slice(side * HALF + b * 256, side * HALF + (b + 1) * 256)
                normed = n[rows, :]
                gate = nt(wgu[gate_rows, :], normed)
                up = nt(wgu[up_rows, :], normed)
                grad = nt(wd[down_rows, :], cot[rows, :])
                sig = 1.0 / (1.0 + jnp.exp(-gate))
                silu = gate * sig
                act[down_rows, cols] = (silu * up).astype(BF)
                dgu[gate_rows, cols] = (grad * up * sig * (1.0 + gate * (1.0 - sig))).astype(BF)
                dgu[up_rows, cols] = (grad * silu).astype(BF)
        both = pl.ds(pl.multiple_of(j * (2 * HID), 32), 2 * HID)
        half = RB // 2
        rest = 2 * HID - half
        for k in (3, 1, 2, 0):
            one, two = slot_of(0, k), slot_of(1, k)
            g = nn(dgu[both, 0:HALF], n_own[:, lanes(k)]) + nn(dgu[both, HALF:LEN], n_oth[:, lanes(k)])
            chunk[j, 0, one, :, :] = g[0:half].astype(BF)
            chunk[j, 1, two, 0:rest, :] = g[half:].astype(BF)
            if k == 0:
                plane.start(j)
            g = nn(act[down_rows, 0:HALF], cot_own[:, lanes(k)]) + nn(act[down_rows, HALF:LEN], cot_oth[:, lanes(k)])
            chunk[j, 1, two, rest:half, :] = g.astype(BF)

        @pl.when(i == 2)
        def _():
            plane.stage2(1)

        @pl.when(i == 3)
        def _():
            plane.stage2(3)

        return carry

    lax.fori_loop(0, 4, feed, 0)
    own, oth = slice(0, HALF), slice(HALF, LEN)
    d_send[...] = tn(dgu[:, oth], wgu[...]).astype(BF)
    sends.go(d_send, d_got, pair_send.at[0], pair_recv.at[0], partner)
    y_send[...] = tn(act[:, oth], wd[...]).astype(BF)
    sends.go(y_send, y_got, pair_send.at[1], pair_recv.at[1], partner)
    arrived(d_got, pair_recv.at[0], None)
    gain = local_gain(gain_f)
    total = jnp.zeros((1, D), F32)
    for b in range(2):
        rows = slice(b * 256, (b + 1) * 256)
        grad = tn(dgu[:, rows], wgu[...]) + d_got[rows, :].astype(F32)
        back, part = norm_back(grad, hidden[rows, :], gain)
        total = total + part
        g = cot_own[rows, :].astype(F32) + back
        grad_hidden[rows, :] = g
        low_own[rows, :] = g.astype(BF)
    put_gain(gain_two, 0, total)
    sends.go(low_own, low_oth, pair_send.at[2], pair_recv.at[2], partner)
    arrived(y_got, pair_recv.at[1], None)
    for b in range(2):
        rows = slice(b * 256, (b + 1) * 256)
        rows_buf[rows, :] = (hidden[rows, :] + (tn(act[:, rows], wd[...]) + y_got[rows, :].astype(F32))).astype(BF)
    rows_back(sends, rows_buf, out_rows, row_send, row_recv)
    plane.stage2(2)
    plane.stage3(1, z_out.at[0])
    plane.stage2(0)
    sends.go(z_out.at[0], z_in.at[0], z_send.at[0], z_recv.at[0], at(q, c, t ^ 1))
    plane.stage3(3, z_out.at[1])
    plane.stage3(2, sums.at[1])
    sends.go(z_out.at[1], z_in.at[1], z_send.at[1], z_recv.at[1], at(q, c, t ^ 1))
    plane.stage3(0, sums.at[0])
    for i in range(2):
        arrived(z_in.at[i], z_recv.at[i], None)
        sums[i] = add_low(sums[i], z_in[i])
    arrived(low_oth, pair_recv.at[2], None)
    rows_back_in(out_rows, row_recv)
    plane.drain()
    sends.drain()


def middle(*args):
    half16 = ((HALF, D), BF, VM)
    outs = [((2, RB, DP), BF, VM), ((HALF, D), F32, VM), half16, half16, ((MICRO, 256, D), BF, VM), ((1, D), F32, VM)]
    buf = pltpu.VMEM((HALF, D), BF)
    scratch = [
        pltpu.VMEM((4 * 2 * HID, D), BF), pltpu.VMEM((4 * HID, D), BF), pltpu.VMEM((4 * HID, LEN), BF),
        pltpu.VMEM((4 * 2 * HID, LEN), BF), pltpu.VMEM((4, 2, NQ, RB // 2, DP), BF), pltpu.VMEM((4, 2, 2, RB // 2, DP), BF),
        pltpu.VMEM((4, 2, RB // 2, DP), BF), pltpu.VMEM((2, RB, DP), BF), pltpu.VMEM((2, RB, DP), BF), buf, buf, buf, buf, buf,
        DMA((3, 4)), DMA((3, 2)), DMA((4, 2)), DMA((4, 2)), DMA((4, 2)), DMA((4, 2)), DMA((2,)), DMA((2,)), DMA((3,)), DMA((3,)),
        DMA((2, 4)), DMA((2, 4)),
    ]
    return remote_call(middle_body, "middle", 1, args, [VM] * 6 + [HBM] * 4, outs, scratch, 2.6e10)


class Spread:
    def __init__(self, piece, got, sends, send_sem, recv_sem):
        self.piece, self.got, self.sends, self.ss, self.rs = piece, got, sends, send_sem, recv_sem
        _, self.q, self.c, self.t = where_am_i()

    def place(self, k, half, p=None):
        size = self.got.shape[1] // 2
        rows = pl.ds(0, 2 * size) if p is None else pl.ds(p * size, size)
        return self.got.at[half, rows, block(self.q ^ k, DP)]

    def go(self, src, dst, number, device):
        self.sends.go(src, dst, self.ss.at[number], self.rs.at[number], device)

    def start(self):
        q, c, t = self.q, self.c, self.t
        for k in (1, 2):
            self.go(self.piece, self.place(0, c), k, at(q ^ k, c, t))
        self.go(self.piece, self.place(0, c), 4, at(q, 1 - c, t))
        pltpu.make_async_copy(self.piece, self.place(0, c), self.rs.at[0]).start()

    def relay(self):
        q, c, t = self.q, self.c, self.t
        for p, k, number in ((0, 1, 3), (1, 2, 8)):
            arrived(self.place(k, c), self.rs.at[k], None)
            self.go(self.place(k, c, p), self.place(k, c, p), number, at(q ^ (3 - k), c, t))
            self.go(self.place(k, c), self.place(k, c), 4 + k, at(q, 1 - c, t))

    def last(self):
        for p, number in ((0, 3), (1, 8)):
            arrived(self.place(3, self.c, p), self.rs.at[number], None)
        self.go(self.place(3, self.c), self.place(3, self.c), 7, at(self.q, 1 - self.c, self.t))

    def finish(self):
        arrived(self.place(0, self.c), self.rs.at[0], None)
        for k in range(NQ):
            arrived(self.place(k, 1 - self.c), self.rs.at[4 + k], None)


def tail_body(low_own, low_oth, n_own, n_oth, x_own, wa, qkv_all, att_all, lse_all, mem_all, grad_hidden, gain_a, gain_two,
              sums_b, grad_rows, got_b, got_a, gains,
              da, dk, dv, dall, chunk, recv1, recv2, sums_a, zb, z1, z2, piece_b, piece_a, d_send, d_got, rows_buf, g_near, g_far,
              s1, r1, s2, r2, zb_send, zb_recv, z1_send, z1_recv, z2_send, z2_recv, pair_send, pair_recv, row_send, row_recv,
              bs, br, as_, ar, gs, gr, hs, hr):
    _, q, c, t = where_am_i()
    sends = Sends()
    greet(everyone(q, c, t) + [at(q ^ 3, c, t)])
    plane = Plane(chunk, recv1, recv2, (s1, r1, s2, r2))
    sends.go(sums_b.at[1], zb, zb_send.at[0], zb_recv.at[0], at(q, c, t ^ 2))

    def z_first(i):
        sends.go(sums_a.at[2 * i + 1], z1.at[i], z1_send.at[i], z1_recv.at[i], at(q, c, t ^ 1))

    def attend_back(i, carry):
        j = turn(i)
        wo = wa[j, 3 * HD : 4 * HD, :]
        qkv, lse, mem, head = qkv_all.at[j], lse_all.at[j], mem_all.at[j], block(j, HD)
        grad_o = jnp.zeros((HD, D), F32)
        for who, g in ((c, low_own), (1 - c, low_oth)):
            rows = block(who, HALF)
            grads = g[...]
            da[rows, :] = nt(grads, wo).astype(BF)
            grad_o = grad_o + tn(att_all[rows, head], grads)
        keep = causal()
        for b in range(LEN // BLK):
            rows = slice(b * BLK, (b + 1) * BLK)
            query = qkv[rows, 0:HD]
            grad = da[rows, :]
            level = lse[rows, 0:1]
            mem_k = mem[b * TOPK : (b + 1) * TOPK, :]
            mem_v = mem[512 + b * TOPK : 512 + (b + 1) * TOPK, :]
            p_d = jnp.exp(jnp.where(keep, nt(query, qkv[rows, HD : 2 * HD]), NEG) - level)
            p_f = jnp.exp(nt(query, mem_k) - level)
            g_d = nt(grad, qkv[rows, 2 * HD : 3 * HD])
            g_f = nt(grad, mem_v)
            delta = jnp.sum(p_d * g_d, axis=1, keepdims=True) + jnp.sum(p_f * g_f, axis=1, keepdims=True)
            if b:
                past = slice(0, b * BLK)
                p_p = jnp.exp(nt(query, qkv[past, HD : 2 * HD]) - level)
                g_p = nt(grad, qkv[past, 2 * HD : 3 * HD])
                delta = delta + jnp.sum(p_p * g_p, axis=1, keepdims=True)
            s_d = (p_d * (g_d - delta)).astype(BF)
            s_f = (p_f * (g_f - delta)).astype(BF)
            dq = nn(s_d, qkv[rows, HD : 2 * HD]) + nn(s_f, mem_k)
            if b:
                s_p = (p_p * (g_p - delta)).astype(BF)
                dq = dq + nn(s_p, qkv[past, HD : 2 * HD])
                dk[past, :] = dk[past, :] + tn(s_p, query)
                dv[past, :] = dv[past, :] + tn(p_p.astype(BF), grad)
            dk[rows, :] = tn(s_d, query)
            dv[rows, :] = tn(p_d.astype(BF), grad)
            dall[j, rows, 0:HD] = (dq * (HD**-0.5)).astype(BF)
        dall[j, :, HD : 2 * HD] = dk[...].astype(BF)
        dall[j, :, 2 * HD : 3 * HD] = dv[...].astype(BF)
        grad_w = tn(dall[j, block(c, HALF), :], n_own[...]) + tn(dall[j, block(1 - c, HALF), :], n_oth[...])
        for k in range(NQ):
            one, two = slot_of(0, k), slot_of(1, k)
            chunk[j, 0, one, :, :] = grad_w[0 : 2 * HD, lanes(k)].astype(BF)
            chunk[j, 1, two, 0:HD, :] = grad_w[2 * HD : 3 * HD, lanes(k)].astype(BF)
            chunk[j, 1, two, HD : 2 * HD, :] = grad_o[:, lanes(k)].astype(BF)

        @pl.when(i >= 1)
        def _():
            plane.stage2(turn(i - 1))

        plane.start(j)
        return carry

    lax.fori_loop(0, 4, attend_back, 0)
    weights = jnp.concatenate([wa[j, 0 : 3 * HD, :] for j in range(4)], axis=0)

    def into_rows(who, b):
        rows = pl.ds(pl.multiple_of(who * HALF + b * 256, 256), 256)
        d = jnp.concatenate([dall[j, rows, :] for j in range(4)], axis=1)
        return nn(d, weights)

    for b in range(2):
        d_send[b * 256 : (b + 1) * 256, :] = into_rows(1 - c, b).astype(BF)
    sends.go(d_send, d_got, pair_send.at[0], pair_recv.at[0], at(q, 1 - c, t))
    plane.stage3(1, sums_a.at[1])
    plane.stage3(3, sums_a.at[3])
    z_first(0)
    arrived(d_got, pair_recv.at[0], None)
    to_b = Spread(piece_b, got_b, sends, bs, br)
    to_a = Spread(piece_a, got_a, sends, as_, ar)
    gain = local_gain(gain_a)
    total = jnp.zeros((1, D), F32)
    for b in range(2):
        rows = slice(b * 256, (b + 1) * 256)
        grad = into_rows(c, b) + d_got[rows, :].astype(F32)
        back, part = norm_back(grad, x_own[rows, :].astype(F32), gain)
        total = total + part
        rows_buf[rows, :] = (grad_hidden[rows, :] + back).astype(BF)
        if b == 0:
            z_first(1)
            plane.stage2(0)
            arrived(zb, zb_recv.at[0], None)
            piece_b[...] = add_low(sums_b[0], zb[...])
            to_b.start()
    here = c * 4 + t
    put_gain(g_near.at[here], 0, total)
    g_near[here, 1:2, :] = gain_two[...]
    group = [(dc, dt) for dc in range(2) for dt in range(4) if dc + dt]
    for i, (dc, dt) in enumerate(group):
        sends.go(g_near.at[here], g_near.at[here], gs.at[i], gr.at[here], at(q, c ^ dc, t ^ dt))
    rows_back(sends, rows_buf, grad_rows, row_send, row_recv, (0,))
    plane.stage3(2, sums_a.at[2])
    arrived(z1.at[1], z1_recv.at[1], None)
    sums_a[2] = add_low(sums_a[2], z1[1])
    for dc, dt in group:
        there = (c ^ dc) * 4 + (t ^ dt)
        arrived(g_near.at[there], gr.at[there], None)
    sends.go(sums_a.at[2], z2, z2_send.at[0], z2_recv.at[0], at(q, c, t ^ 2))
    rows_back(sends, rows_buf, grad_rows, row_send, row_recv, (1,))
    part = g_near[0]
    for i in range(1, 8):
        part = part + g_near[i]
    g_far[q] = part
    for k in range(1, NQ):
        sends.go(g_far.at[q], g_far.at[q], hs.at[k], hr.at[q], at(q ^ k, c, t))
    plane.stage3(0, sums_a.at[0])
    to_b.relay()
    arrived(z1.at[0], z1_recv.at[0], None)
    arrived(z2, z2_recv.at[0], None)
    piece_a[...] = ((sums_a[0].astype(F32) + z1[0].astype(F32)) + z2[...].astype(F32)).astype(BF)
    to_a.start()
    to_b.last()
    for k in range(1, NQ):
        arrived(g_far.at[q ^ k], hr.at[q ^ k], None)
    gains[...] = ((g_far[0] + g_far[1]) + g_far[2]) + g_far[3]
    to_a.relay()
    to_a.last()
    to_b.finish()
    to_a.finish()
    rows_back_in(grad_rows, row_recv)
    plane.drain()
    sends.drain()


def tail(*args):
    outs = [((MICRO, 256, D), BF, VM), ((2, RB, D), BF, HBM), ((2, RA, D), BF, HBM), ((2, D), F32, VM)]
    buf = pltpu.VMEM((HALF, D), BF)
    scratch = [
        pltpu.VMEM((LEN, HD), BF), pltpu.VMEM((LEN, HD), F32), pltpu.VMEM((LEN, HD), F32), pltpu.VMEM((4, LEN, 3 * HD), BF),
        pltpu.VMEM((4, 2, NQ, RA // 2, DP), BF), pltpu.VMEM((4, 2, 2, RA // 2, DP), BF), pltpu.VMEM((4, 2, RA // 2, DP), BF),
        pltpu.VMEM((4, RA, DP), BF), pltpu.VMEM((RB, DP), BF), pltpu.VMEM((2, RA, DP), BF), pltpu.VMEM((RA, DP), BF),
        pltpu.VMEM((RB, DP), BF), pltpu.VMEM((RA, DP), BF), buf, buf, buf,
        pltpu.VMEM((8, 2, D), F32), pltpu.VMEM((NQ, 2, D), F32),
        DMA((4, 2)), DMA((4, 2)), DMA((4, 2)), DMA((4, 2)), DMA((1,)), DMA((1,)), DMA((2,)), DMA((2,)), DMA((1,)), DMA((1,)),
        DMA((1,)), DMA((1,)), DMA((2, 4)), DMA((2, 4)), DMA((9,)), DMA((9,)), DMA((9,)), DMA((9,)), DMA((7,)), DMA((8,)),
        DMA((4,)), DMA((4,)),
    ]
    return remote_call(tail_body, "tail", 2, args, [VM] * 14, outs, scratch, 1.5e10)


def per_device(tokens, attn_gain, ffn_gain, query_weight, key_weight, value_weight, out_weight, gate_weight,
               up_weight, down_weight, cache_keys, cache_values, knn_index, cotangent):
    gain_a, gain_f = attn_gain.reshape(1, D), ffn_gain.reshape(1, D)
    gate_t, up_t = gate_weight.T, up_weight.T
    wa, wb, x_own, n1_own, n1_oth, cot_own, cot_oth, mem, qkv, att, lse, hidden, n2_own, n2_oth = front(
        tokens, cotangent, gain_a, gain_f, cache_keys, cache_values, knn_index, query_weight, key_weight, value_weight,
        out_weight, gate_t, up_t, down_weight,
    )
    sums_b, grad_hidden, low_own, low_oth, output, gain_two = middle(
        n2_own, n2_oth, cot_own, cot_oth, hidden, gain_f, gate_t, up_t, down_weight, wb
    )
    grad_tokens, got_b, got_a, gains = tail(
        low_own, low_oth, n1_own, n1_oth, x_own, wa, qkv, att, lse, mem, grad_hidden, gain_a, gain_two, sums_b
    )
    if lax.axis_size("r") > 1:
        got_b = lax.psum(got_b.astype(F32), "r")
        got_a = lax.psum(got_a.astype(F32), "r")
        gains = lax.psum(gains, "r")
    tall = ((2 * HID, D), F32)
    gg, gu, gd = call(place_b_body, [tall, tall, tall], (got_b,), name="place_b")
    col, row = ((D, 2 * HD), F32), ((2 * HD, D), F32)
    gq, gk, gv, go = call(place_a_body, [col, col, col, row], (got_a,), name="place_a")
    return output, grad_tokens, gq, gk, gv, go, gg.T, gu.T, gd, gains[0], gains[1]


def solution(mesh):
    n_dp, n_t = mesh.shape["dp"], mesh.shape["tensor"]
    fine = Mesh(mesh.devices.reshape(n_dp // 8, NQ, 2, n_t), ("r", "q", "c", "t"))
    dp = ("r", "q", "c")
    rows = P(None, dp + ("t",), None)
    placed = (
        rows, P(), P(), P(None, "t"), P(None, "t"), P(None, "t"), P("t", None), P(None, "t"), P(None, "t"),
        P("t", None), P(None, dp, "t"), P(None, dp, "t"), P(None, dp, "t", None), rows,
    )
    return jax.shard_map(
        per_device,
        mesh=fine,
        in_specs=placed,
        out_specs=(
            rows, rows, P(None, "t"), P(None, "t"), P(None, "t"), P("t", None), P(None, "t"), P(None, "t"),
            P("t", None), P(), P(),
        ),
        check_vma=False,
    )
```

profile of v0, /device:TPU:0, one launch (start us, length us, event | category | flops | bytes accessed | tf_op | source)
XLA Modules:
  0.0 357.3 jit_solution(7640218863922389737)
XLA Ops:
  0.6 132.9 %front.1 = (bf16[4,512,1024]{2,1,0:T(8,128)(2,1)}, bf16[3,1056,1024]{2,1,0:T(8,128)(2,1)}, bf16[512,1024]{1,0:T(8,128)(2,1)}, bf16[512,1024]{1,0:T(8,128)(2,1)},...) custom-call(bf16[2,256,1024]{2,1,0:T(8,128)(2,1)} %tok.1, ...), custom_call_target="tpu_custom_call" | custom-call | flops 20000000000 | bytes 50000000 | tf_op jit(solution)/shard_map/front/pallas_call | solution.py:386
  133.5 106.5 %middle.1 = (bf16[2,1056,256]{2,1,0:T(8,128)(2,1)}, f32[512,1024]{1,0:T(8,128)}, bf16[512,1024]{1,0:T(8,128)(2,1)}, bf16[512,1024]{1,0:T(8,128)(2,1)}, bf16[2,256,1024]{2,1,0:T(8,128)(2,1)}, /*index=5*/f32[1,1024]{1,0:T(1,128)}) custom-call(bf16[512,1024]{1,0:T(8,128)(2,1)} %get-tuple-element.42.n_own, bf16[512,1024]{1,0:T(8,128)(2,1)} %get-tuple-element.43.n_oth, ...), custom_call_target="tpu_custom_call" | custom-call | flops 25999998976 | bytes 50000000 | tf_op jit(solution)/shard_map/middle/pallas_call | solution.py:499
  240.0 103.2 %tail.1 = (bf16[2,256,1024]{2,1,0:T(8,128)(2,1)}, bf16[2,1056,1024]{2,1,0:T(8,128)(2,1)}, bf16[2,512,1024]{2,1,0:T(8,128)(2,1)}, f32[2,1024]{1,0:T(2,128)}) custom-call(bf16[512,1024]{1,0:T(8,128)(2,1)} %get-tuple-element.49.low_own, bf16[512,1024]{1,0:T(8,128)(2,1)} %get-tuple-element.50.low_oth, bf16[512,1024]{1,0:T(8,128)(2,1)} %get-tuple-element.51.n_own, ...), custom_call_target="tpu_custom_call" | custom-call | flops 15000000512 | bytes 50000000 | tf_op jit(solution)/shard_map/tail/pallas_call | solution.py:499
  343.2 1.4 fusion
  344.6 3.9 %place_a.1 = (f32[1024,256]{1,0:T(8,128)}, f32[1024,256]{1,0:T(8,128)}, f32[1024,256]{1,0:T(8,128)}, f32[256,1024]{1,0:T(8,128)}) custom-call(bf16[2,512,1024]{2,1,0:T(8,128)(2,1)} %get-tuple-element.63.got), custom_call_target="tpu_custom_call" | custom-call | bytes 6291456 | tf_op jit(solution)/shard_map/place_a/pallas_call | solution.py:51
  348.6 0.0 copy-start
  348.6 6.0 %place_b.1 = (f32[704,1024]{1,0:T(8,128)}, f32[704,1024]{1,0:T(8,128)}, f32[704,1024]{1,0:T(8,128)}) custom-call(bf16[2,1056,1024]{2,1,0:T(8,128)(2,1)} %get-tuple-element.68.got), custom_call_target="tpu_custom_call" | custom-call | bytes 12976128 | tf_op jit(solution)/shard_map/place_b/pallas_call | solution.py:51
  354.5 0.0 copy-start.1
  354.5 0.0 copy-done
  354.5 1.0 copy.27
  355.5 0.6 copy-done.1
  356.1 1.0 copy.28
Async XLA Ops:
  348.6 6.0 %copy-start = (bf16[2,256,1024]{2,1,0:T(8,128)(2,1)S(1)}, bf16[2,256,1024]{2,1,0:T(8,128)(2,1)}, u32[]{:S(2)}) copy-start(bf16[2,256,1024]{2,1,0:T(8,128)(2,1)} %get-tuple-element.86) | copy-start | bytes 3145732
  354.5 1.6 copy-start.1
where the time goes:
time: 361 us; the launch traced here: 357 us
  Pallas kernels  352 us (98%)
  local copies, waits for them, and re-layouts  3.95 us (1%)
    pallas_call x2, Pallas kernels, remote_call(): pl.pallas_call(body, out_shape=[jax.ShapeDtypeStruct(s, d) for s, d, _ in...  210 us
    pallas_call x1, Pallas kernels, front(): pl.pallas_call(front_body, out_shape=[jax.ShapeDtypeStruct(s, d) for s, d...  133 us
    pallas_call x2, Pallas kernels, call(): pl.pallas_call(body, out_shape=[jax.ShapeDtypeStruct(s, t) for s, t in ou...  9.91 us

commit v1 on v0

--- a/solution.py
+++ b/solution.py
@@ -44,22 +44,6 @@
 VM = pl.BlockSpec(memory_space=pltpu.VMEM)
 
 
-def call(body, outs, args, flops=0, trans=0, scratch=(), name=None, vmem=None):
-    nbytes = sum(a.size * a.dtype.itemsize for a in args) + sum(
-        jnp.dtype(t).itemsize * functools.reduce(lambda x, y: x * y, s, 1) for s, t in outs
-    )
-    return pl.pallas_call(
-        body,
-        out_shape=[jax.ShapeDtypeStruct(s, t) for s, t in outs],
-        in_specs=[VM for _ in args],
-        out_specs=[VM for _ in outs],
-        scratch_shapes=list(scratch),
-        name=name,
-        compiler_params=pltpu.CompilerParams(vmem_limit_bytes=vmem),
-        cost_estimate=pl.CostEstimate(flops=int(flops), bytes_accessed=int(nbytes), transcendentals=int(trans)),
-    )(*args)
-
-
 def block(index, size):
     return pl.ds(pl.multiple_of(index * size, size), size)
 
@@ -96,6 +80,24 @@
     for half in range(2):
         for i, out in enumerate(outs):
             out[half * HID : (half + 1) * HID, :] = got[half, i * HID : (i + 1) * HID, :].astype(F32)
+
+
+def place(body, got, kinds, name):
+    shapes = {"tall": (2 * HID, D), "col": (D, 2 * HD), "row": (2 * HD, D)}
+    specs = {
+        "tall": pl.BlockSpec((2 * HID, DP), lambda i: (0, i)),
+        "col": pl.BlockSpec((DP, 2 * HD), lambda i: (i, 0)),
+        "row": pl.BlockSpec((2 * HD, DP), lambda i: (0, i)),
+    }
+    return pl.pallas_call(
+        body,
+        grid=(NQ,),
+        out_shape=[jax.ShapeDtypeStruct(shapes[k], F32) for k in kinds],
+        in_specs=[pl.BlockSpec((*got.shape[:2], DP), lambda i: (0, 0, i))],
+        out_specs=[specs[k] for k in kinds],
+        name=name,
+        cost_estimate=pl.CostEstimate(flops=0, bytes_accessed=int(got.size * 6), transcendentals=0),
+    )(got)
 
 
 def where_am_i():
@@ -323,9 +325,6 @@
     def got_mem(j):
         arrived(mem.at[j], mem_recv.at[j], None)
 
-    project(0, c, n_own)
-    arrived(n_oth, pair_recv.at[0], None)
-    project(0, 1 - c, n_oth)
     relay_a(2, 2, ends)
     relay_a(3, 2, mid)
     relay_b(2, 2, ends)
@@ -333,27 +332,22 @@
     send_mem()
     rows_out(cot, cot_own, cot_send, cot_recv)
     relay_far(2, a_whole, xa_send, xa_recv)
-    in_place(1, a_whole, xa_recv)
-    project(1, c, n_own)
-    project(1, 1 - c, n_oth)
-    got_mem(0)
-    attend(0)
+    arrived(n_oth, pair_recv.at[0], None)
     relay_far(2, b_whole, xb_send, xb_recv)
     relay_a(3, 3, ends)
     relay_b(3, 3, ends)
-    in_place(2, a_whole, xa_recv)
-    project(second, c, n_own)
-    project(second, 1 - c, n_oth)
-    got_mem(1)
-    attend(1)
-    in_place(3, a_whole, xa_recv)
-    project(third, c, n_own)
-    project(third, 1 - c, n_oth)
-    got_mem(second)
-    attend(second)
-    got_mem(third)
-    attend(third)
-
+
+    def head(i, carry):
+        j = jnp.where(i < 2, i, jnp.where(i == 2, second, third))
+        for order in range(1, 4):
+            pl.when(i == order)(functools.partial(in_place, order, a_whole, xa_recv))
+        project(j, c, n_own)
+        project(j, 1 - c, n_oth)
+        got_mem(j)
+        attend(j)
+        return carry
+
+    lax.fori_loop(0, 4, head, 0)
     weights = jnp.concatenate([wa[j, 3 * HD : 4 * HD, :] for j in range(4)], axis=0)
     o_send[...] = nn(att[block(1 - c, HALF), :], weights).astype(BF)
     sends.go(o_send, o_got, pair_send.at[1], pair_recv.at[1], partner)
@@ -682,13 +676,32 @@
             arrived(self.place(k, 1 - self.c), self.rs.at[4 + k], None)
 
 
-def tail_body(low_own, low_oth, n_own, n_oth, x_own, wa, qkv_all, att_all, lse_all, mem_all, grad_hidden, gain_a, gain_two,
-              sums_b, grad_rows, got_b, got_a, gains,
+def tail_body(low_own, low_oth, gain_a, gain_two, sums_b, n_own_in, n_oth_in, x_in, wa_in, qkv_in, att_in, lse_in, mem_in, gh_in,
+              grad_rows, got_b, got_a, gains,
+              n_own, n_oth, x_own, wa, qkv_all, att_all, lse_all, mem_all, grad_hidden, load_sem, head_sem,
               da, dk, dv, dall, chunk, recv1, recv2, sums_a, zb, z1, z2, piece_b, piece_a, d_send, d_got, rows_buf, g_near, g_far,
               s1, r1, s2, r2, zb_send, zb_recv, z1_send, z1_recv, z2_send, z2_recv, pair_send, pair_recv, row_send, row_recv,
               bs, br, as_, ar, gs, gr, hs, hr):
     _, q, c, t = where_am_i()
     sends = Sends()
+
+    def head_loads(j):
+        for i, (one, two) in enumerate(((wa_in, wa), (qkv_in, qkv_all), (lse_in, lse_all), (mem_in, mem_all))):
+            yield pltpu.make_async_copy(one.at[j], two.at[j], head_sem.at[j, i])
+
+    shared = [
+        pltpu.make_async_copy(one, two, load_sem.at[i])
+        for i, (one, two) in enumerate(
+            ((att_in, att_all), (n_own_in, n_own), (n_oth_in, n_oth), (x_in, x_own), (gh_in, grad_hidden))
+        )
+    ]
+    for copy in shared[:3]:
+        copy.start()
+    for j in (1, 3, 2, 0):
+        for copy in head_loads(j):
+            copy.start()
+    for copy in shared[3:]:
+        copy.start()
     greet(everyone(q, c, t) + [at(q ^ 3, c, t)])
     plane = Plane(chunk, recv1, recv2, (s1, r1, s2, r2))
     sends.go(sums_b.at[1], zb, zb_send.at[0], zb_recv.at[0], at(q, c, t ^ 2))
@@ -698,6 +711,8 @@
 
     def attend_back(i, carry):
         j = turn(i)
+        for copy in head_loads(j):
+            copy.wait()
         wo = wa[j, 3 * HD : 4 * HD, :]
         qkv, lse, mem, head = qkv_all.at[j], lse_all.at[j], mem_all.at[j], block(j, HD)
         grad_o = jnp.zeros((HD, D), F32)
@@ -751,7 +766,11 @@
         plane.start(j)
         return carry
 
+    for copy in shared[:3]:
+        copy.wait()
     lax.fori_loop(0, 4, attend_back, 0)
+    for copy in shared[3:]:
+        copy.wait()
     weights = jnp.concatenate([wa[j, 0 : 3 * HD, :] for j in range(4)], axis=0)
 
     def into_rows(who, b):
@@ -826,6 +845,8 @@
     outs = [((MICRO, 256, D), BF, VM), ((2, RB, D), BF, HBM), ((2, RA, D), BF, HBM), ((2, D), F32, VM)]
     buf = pltpu.VMEM((HALF, D), BF)
     scratch = [
+        buf, buf, buf, pltpu.VMEM((4, RA, D), BF), pltpu.VMEM((4, LEN, 3 * HD), BF), pltpu.VMEM((LEN, 4 * HD), BF),
+        pltpu.VMEM((4, LEN, HD), F32), pltpu.VMEM((4, 1024, HD), BF), pltpu.VMEM((HALF, D), F32), DMA((5,)), DMA((4, 4)),
         pltpu.VMEM((LEN, HD), BF), pltpu.VMEM((LEN, HD), F32), pltpu.VMEM((LEN, HD), F32), pltpu.VMEM((4, LEN, 3 * HD), BF),
         pltpu.VMEM((4, 2, NQ, RA // 2, DP), BF), pltpu.VMEM((4, 2, 2, RA // 2, DP), BF), pltpu.VMEM((4, 2, RA // 2, DP), BF),
         pltpu.VMEM((4, RA, DP), BF), pltpu.VMEM((RB, DP), BF), pltpu.VMEM((2, RA, DP), BF), pltpu.VMEM((RA, DP), BF),
@@ -835,7 +856,7 @@
         DMA((1,)), DMA((1,)), DMA((2, 4)), DMA((2, 4)), DMA((9,)), DMA((9,)), DMA((9,)), DMA((9,)), DMA((7,)), DMA((8,)),
         DMA((4,)), DMA((4,)),
     ]
-    return remote_call(tail_body, "tail", 2, args, [VM] * 14, outs, scratch, 1.5e10)
+    return remote_call(tail_body, "tail", 2, args, [VM] * 5 + [HBM] * 9, outs, scratch, 1.5e10)
 
 
 def per_device(tokens, attn_gain, ffn_gain, query_weight, key_weight, value_weight, out_weight, gate_weight,
@@ -850,16 +871,14 @@
         n2_own, n2_oth, cot_own, cot_oth, hidden, gain_f, gate_t, up_t, down_weight, wb
     )
     grad_tokens, got_b, got_a, gains = tail(
-        low_own, low_oth, n1_own, n1_oth, x_own, wa, qkv, att, lse, mem, grad_hidden, gain_a, gain_two, sums_b
+        low_own, low_oth, gain_a, gain_two, sums_b, n1_own, n1_oth, x_own, wa, qkv, att, lse, mem, grad_hidden
     )
     if lax.axis_size("r") > 1:
         got_b = lax.psum(got_b.astype(F32), "r")
         got_a = lax.psum(got_a.astype(F32), "r")
         gains = lax.psum(gains, "r")
-    tall = ((2 * HID, D), F32)
-    gg, gu, gd = call(place_b_body, [tall, tall, tall], (got_b,), name="place_b")
-    col, row = ((D, 2 * HD), F32), ((2 * HD, D), F32)
-    gq, gk, gv, go = call(place_a_body, [col, col, col, row], (got_a,), name="place_a")
+    gg, gu, gd = place(place_b_body, got_b, ("tall", "tall", "tall"), "place_b")
+    gq, gk, gv, go = place(place_a_body, got_a, ("col", "col", "col", "row"), "place_a")
     return output, grad_tokens, gq, gk, gv, go, gg.T, gu.T, gd, gains[0], gains[1]
 
 

time: 361 us -> 352 us (0.975); the launches traced: 357 us -> 352 us
  Pallas kernels: 352 us -> 347 us
    pallas_call x2, Pallas kernels: 210 us -> 206 us  [remote_call(): pl.pallas_call(body, out_shape=[jax.ShapeDtypeStruct(s, d) for s, d, _ in...]
where the time goes in v1:
time: 352 us
  Pallas kernels  347 us (99%)
  local copies, waits for them, and re-layouts  3.95 us (1%)
    pallas_call x2, Pallas kernels, remote_call(): pl.pallas_call(body, out_shape=[jax.ShapeDtypeStruct(s, d) for s, d, _ in...  206 us
    pallas_call x1, Pallas kernels, front(): pl.pallas_call(front_body, out_shape=[jax.ShapeDtypeStruct(s, d) for s, d...  132 us
    pallas_call x2, Pallas kernels, place(): pl.pallas_call(body, grid=(NQ,), out_shape=[jax.ShapeDtypeStruct(shapes[k...  10.4 us

profile of v1, /device:TPU:0, one launch (start us, length us, event | category | flops | bytes accessed | tf_op | source)
XLA Modules:
  0.0 352.0 jit_solution(15583222952733389363)
XLA Ops:
  0.6 131.5 %front.1 = (bf16[4,512,1024]{2,1,0:T(8,128)(2,1)}, bf16[3,1056,1024]{2,1,0:T(8,128)(2,1)}, bf16[512,1024]{1,0:T(8,128)(2,1)}, bf16[512,1024]{1,0:T(8,128)(2,1)},...) custom-call(bf16[2,256,1024]{2,1,0:T(8,128)(2,1)} %tok.1, ...), custom_call_target="tpu_custom_call" | custom-call | flops 20000000000 | bytes 50000000 | tf_op jit(solution)/shard_map/front/pallas_call | solution.py:380
  132.2 105.3 %middle.1 = (bf16[2,1056,256]{2,1,0:T(8,128)(2,1)}, f32[512,1024]{1,0:T(8,128)}, bf16[512,1024]{1,0:T(8,128)(2,1)}, bf16[512,1024]{1,0:T(8,128)(2,1)}, bf16[2,256,1024]{2,1,0:T(8,128)(2,1)}, /*index=5*/f32[1,1024]{1,0:T(1,128)}) custom-call(bf16[512,1024]{1,0:T(8,128)(2,1)} %get-tuple-element.42.n_own, bf16[512,1024]{1,0:T(8,128)(2,1)} %get-tuple-element.43.n_oth, ...), custom_call_target="tpu_custom_call" | custom-call | flops 25999998976 | bytes 50000000 | tf_op jit(solution)/shard_map/middle/pallas_call | solution.py:493
  237.5 100.2 %tail.1 = (bf16[2,256,1024]{2,1,0:T(8,128)(2,1)}, bf16[2,1056,1024]{2,1,0:T(8,128)(2,1)}, bf16[2,512,1024]{2,1,0:T(8,128)(2,1)}, f32[2,1024]{1,0:T(2,128)}) custom-call(bf16[512,1024]{1,0:T(8,128)(2,1)} %get-tuple-element.49.low_own, bf16[512,1024]{1,0:T(8,128)(2,1)} %get-tuple-element.50.low_oth, f32[1,1024]{1,0:T(1,128)} %bitcast.19, ...), custom_call_target="tpu_custom_call" | custom-call | flops 15000000512 | bytes 50000000 | tf_op jit(solution)/shard_map/tail/pallas_call | solution.py:493
  337.7 1.4 fusion
  339.1 4.3 %place_a.1 = (f32[1024,256]{1,0:T(8,128)}, f32[1024,256]{1,0:T(8,128)}, f32[1024,256]{1,0:T(8,128)}, f32[256,1024]{1,0:T(8,128)}) custom-call(bf16[2,512,1024]{2,1,0:T(8,128)(2,1)} %get-tuple-element.63.got), custom_call_target="tpu_custom_call" | custom-call | bytes 6291456 | tf_op jit(solution)/shard_map/place_a/pallas_call | solution.py:92
  343.4 0.0 copy-start
  343.4 6.1 %place_b.1 = (f32[704,1024]{1,0:T(8,128)}, f32[704,1024]{1,0:T(8,128)}, f32[704,1024]{1,0:T(8,128)}) custom-call(bf16[2,1056,1024]{2,1,0:T(8,128)(2,1)} %get-tuple-element.68.got), custom_call_target="tpu_custom_call" | custom-call | bytes 12976128 | tf_op jit(solution)/shard_map/place_b/pallas_call | solution.py:92
  349.5 0.0 copy-start.1
  349.5 0.0 copy-done
  349.5 1.0 copy.27
  350.4 0.6 copy-done.1
  351.1 1.0 copy.28
Async XLA Ops:
  343.4 6.1 %copy-start = (bf16[2,256,1024]{2,1,0:T(8,128)(2,1)S(1)}, bf16[2,256,1024]{2,1,0:T(8,128)(2,1)}, u32[]{:S(2)}) copy-start(bf16[2,256,1024]{2,1,0:T(8,128)(2,1)} %get-tuple-element.86) | copy-start | bytes 3145732
  349.5 1.6 copy-start.1

commit v2 on v1

--- a/solution.py
+++ b/solution.py
@@ -349,23 +349,30 @@
 
     lax.fori_loop(0, 4, head, 0)
     weights = jnp.concatenate([wa[j, 3 * HD : 4 * HD, :] for j in range(4)], axis=0)
-    o_send[...] = nn(att[block(1 - c, HALF), :], weights).astype(BF)
-    sends.go(o_send, o_got, pair_send.at[1], pair_recv.at[1], partner)
+    for b in range(2):
+        rows = slice(b * 256, (b + 1) * 256)
+        o_send[rows, :] = nn(att[block(2 * (1 - c) + b, 256), :], weights).astype(BF)
+        sends.go(o_send.at[rows], o_got.at[rows], pair_send.at[1 + b], pair_recv.at[1 + b], partner)
     hidden[...] = nn(att[block(c, HALF), :], weights)
-    rows_in(cot_own, cot_recv)
-    sends.go(cot_own, cot_oth, pair_send.at[2], pair_recv.at[2], partner)
-    arrived(o_got, pair_recv.at[1], None)
     gain = jnp.concatenate([gain_f[:, block(q ^ k, DP)] for k in range(NQ)], axis=1)
-    for i in range(2):
-        rows = slice(i * 256, (i + 1) * 256)
+    for b in range(2):
+        rows = slice(b * 256, (b + 1) * 256)
+        arrived(o_got.at[rows], pair_recv.at[1 + b], None)
         h = x_own[rows, :].astype(F32) + (hidden[rows, :] + o_got[rows, :].astype(F32))
         hidden[rows, :] = h
         n2_own[rows, :] = (h * scale_of(h) * gain).astype(BF)
-    sends.go(n2_own, n2_oth, pair_send.at[3], pair_recv.at[3], partner)
+        sends.go(n2_own.at[rows], n2_oth.at[rows], pair_send.at[3 + b], pair_recv.at[3 + b], partner)
+    for b in range(2):
+        rows = slice(b * 256, (b + 1) * 256)
+        for k in range(NQ):
+            arrived(cot_own.at[rows, lanes(k)], cot_recv.at[b, k], None)
+        sends.go(cot_own.at[rows], cot_oth.at[rows], pair_send.at[5 + b], pair_recv.at[5 + b], partner)
     for order in range(1, 4):
         in_place(order, b_whole, xb_recv)
-    arrived(n2_oth, pair_recv.at[3], None)
-    arrived(cot_oth, pair_recv.at[2], None)
+    for b in range(2):
+        rows = slice(b * 256, (b + 1) * 256)
+        arrived(n2_oth.at[rows], pair_recv.at[3 + b], None)
+        arrived(cot_oth.at[rows], pair_recv.at[5 + b], None)
     sends.drain()
 
 
@@ -387,7 +394,7 @@
             pltpu.VMEM((MICRO, 2, 1024, HD), BF), pltpu.VMEM((HALF, D), BF), pltpu.VMEM((HALF, D), BF),
             dma((2, 4)), dma((2, 4)), dma((2, 4)), dma((2, 4)), dma((2,)), dma((2,)), dma((2, 2)), dma((4,)),
             dma((5, 1)), dma((4, 1)), dma((4, 4)), dma((4, 4)), dma((5, 3)), dma((4, 3)), dma((4, 4)), dma((4, 4)),
-            dma((4,)), dma((4,)),
+            dma((7,)), dma((7,)),
         ],
         compiler_params=pltpu.CompilerParams(collective_id=0, has_side_effects=True, vmem_limit_bytes=60 << 20),
         name="front",

time: 352 us -> 353 us (level)
  no operation moved by 1% of the time
where the time goes in v2:
time: 353 us; the launch traced here: 352 us
  Pallas kernels  348 us (99%)
  local copies, waits for them, and re-layouts  3.95 us (1%)
    pallas_call x2, Pallas kernels, remote_call(): pl.pallas_call(body, out_shape=[jax.ShapeDtypeStruct(s, d) for s, d, _ in...  206 us
    pallas_call x1, Pallas kernels, front(): pl.pallas_call(front_body, out_shape=[jax.ShapeDtypeStruct(s, d) for s, d...  132 us
    pallas_call x2, Pallas kernels, place(): pl.pallas_call(body, grid=(NQ,), out_shape=[jax.ShapeDtypeStruct(shapes[k...  10.4 us

profile of v2, /device:TPU:0, one launch (start us, length us, event | category | flops | bytes accessed | tf_op | source)
XLA Modules:
  0.0 352.2 jit_solution(10634825523374166421)
XLA Ops:
  0.6 131.6 %front.1 = (bf16[4,512,1024]{2,1,0:T(8,128)(2,1)}, bf16[3,1056,1024]{2,1,0:T(8,128)(2,1)}, bf16[512,1024]{1,0:T(8,128)(2,1)}, bf16[512,1024]{1,0:T(8,128)(2,1)},...) custom-call(bf16[2,256,1024]{2,1,0:T(8,128)(2,1)} %tok.1, ...), custom_call_target="tpu_custom_call" | custom-call | flops 20000000000 | bytes 50000000 | tf_op jit(solution)/shard_map/front/pallas_call | solution.py:387
  132.2 105.3 %middle.1 = (bf16[2,1056,256]{2,1,0:T(8,128)(2,1)}, f32[512,1024]{1,0:T(8,128)}, bf16[512,1024]{1,0:T(8,128)(2,1)}, bf16[512,1024]{1,0:T(8,128)(2,1)}, bf16[2,256,1024]{2,1,0:T(8,128)(2,1)}, /*index=5*/f32[1,1024]{1,0:T(1,128)}) custom-call(bf16[512,1024]{1,0:T(8,128)(2,1)} %get-tuple-element.42.n_own, bf16[512,1024]{1,0:T(8,128)(2,1)} %get-tuple-element.43.n_oth, ...), custom_call_target="tpu_custom_call" | custom-call | flops 25999998976 | bytes 50000000 | tf_op jit(solution)/shard_map/middle/pallas_call | solution.py:500
  237.5 100.3 %tail.1 = (bf16[2,256,1024]{2,1,0:T(8,128)(2,1)}, bf16[2,1056,1024]{2,1,0:T(8,128)(2,1)}, bf16[2,512,1024]{2,1,0:T(8,128)(2,1)}, f32[2,1024]{1,0:T(2,128)}) custom-call(bf16[512,1024]{1,0:T(8,128)(2,1)} %get-tuple-element.49.low_own, bf16[512,1024]{1,0:T(8,128)(2,1)} %get-tuple-element.50.low_oth, f32[1,1024]{1,0:T(1,128)} %bitcast.19, ...), custom_call_target="tpu_custom_call" | custom-call | flops 15000000512 | bytes 50000000 | tf_op jit(solution)/shard_map/tail/pallas_call | solution.py:500
  337.9 1.4 fusion
  339.2 4.3 %place_a.1 = (f32[1024,256]{1,0:T(8,128)}, f32[1024,256]{1,0:T(8,128)}, f32[1024,256]{1,0:T(8,128)}, f32[256,1024]{1,0:T(8,128)}) custom-call(bf16[2,512,1024]{2,1,0:T(8,128)(2,1)} %get-tuple-element.63.got), custom_call_target="tpu_custom_call" | custom-call | bytes 6291456 | tf_op jit(solution)/shard_map/place_a/pallas_call | solution.py:92
  343.5 0.0 copy-start
  343.5 6.1 %place_b.1 = (f32[704,1024]{1,0:T(8,128)}, f32[704,1024]{1,0:T(8,128)}, f32[704,1024]{1,0:T(8,128)}) custom-call(bf16[2,1056,1024]{2,1,0:T(8,128)(2,1)} %get-tuple-element.68.got), custom_call_target="tpu_custom_call" | custom-call | bytes 12976128 | tf_op jit(solution)/shard_map/place_b/pallas_call | solution.py:92
  349.6 0.0 copy-start.1
  349.6 0.0 copy-done
  349.6 1.0 copy.27
  350.6 0.6 copy-done.1
  351.2 1.0 copy.28
Async XLA Ops:
  343.5 6.1 %copy-start = (bf16[2,256,1024]{2,1,0:T(8,128)(2,1)S(1)}, bf16[2,256,1024]{2,1,0:T(8,128)(2,1)}, u32[]{:S(2)}) copy-start(bf16[2,256,1024]{2,1,0:T(8,128)(2,1)} %get-tuple-element.86) | copy-start | bytes 3145732
  349.6 1.6 copy-start.1

commit v3 on v2

--- a/solution.py
+++ b/solution.py
@@ -328,8 +328,8 @@
     relay_a(2, 2, ends)
     relay_a(3, 2, mid)
     relay_b(2, 2, ends)
+    send_mem()
     relay_b(3, 2, mid)
-    send_mem()
     rows_out(cot, cot_own, cot_send, cot_recv)
     relay_far(2, a_whole, xa_send, xa_recv)
     arrived(n_oth, pair_recv.at[0], None)

time: 353 us -> 353 us (level)
  no operation moved by 1% of the time
where the time goes in v3:
time: 353 us; the launch traced here: 352 us
  Pallas kernels  348 us (99%)
  local copies, waits for them, and re-layouts  3.95 us (1%)
    pallas_call x2, Pallas kernels, remote_call(): pl.pallas_call(body, out_shape=[jax.ShapeDtypeStruct(s, d) for s, d, _ in...  204 us
    pallas_call x1, Pallas kernels, front(): pl.pallas_call(front_body, out_shape=[jax.ShapeDtypeStruct(s, d) for s, d...  133 us
    pallas_call x2, Pallas kernels, place(): pl.pallas_call(body, grid=(NQ,), out_shape=[jax.ShapeDtypeStruct(shapes[k...  10.4 us

profile of v3, /device:TPU:0, one launch (start us, length us, event | category | flops | bytes accessed | tf_op | source)
XLA Modules:
  0.0 352.1 jit_solution(15572315072144184744)
XLA Ops:
  0.6 132.8 %front.1 = (bf16[4,512,1024]{2,1,0:T(8,128)(2,1)}, bf16[3,1056,1024]{2,1,0:T(8,128)(2,1)}, bf16[512,1024]{1,0:T(8,128)(2,1)}, bf16[512,1024]{1,0:T(8,128)(2,1)},...) custom-call(bf16[2,256,1024]{2,1,0:T(8,128)(2,1)} %tok.1, ...), custom_call_target="tpu_custom_call" | custom-call | flops 20000000000 | bytes 50000000 | tf_op jit(solution)/shard_map/front/pallas_call | solution.py:387
  133.5 104.1 %middle.1 = (bf16[2,1056,256]{2,1,0:T(8,128)(2,1)}, f32[512,1024]{1,0:T(8,128)}, bf16[512,1024]{1,0:T(8,128)(2,1)}, bf16[512,1024]{1,0:T(8,128)(2,1)}, bf16[2,256,1024]{2,1,0:T(8,128)(2,1)}, /*index=5*/f32[1,1024]{1,0:T(1,128)}) custom-call(bf16[512,1024]{1,0:T(8,128)(2,1)} %get-tuple-element.42.n_own, bf16[512,1024]{1,0:T(8,128)(2,1)} %get-tuple-element.43.n_oth, ...), custom_call_target="tpu_custom_call" | custom-call | flops 25999998976 | bytes 50000000 | tf_op jit(solution)/shard_map/middle/pallas_call | solution.py:500
  237.5 100.3 %tail.1 = (bf16[2,256,1024]{2,1,0:T(8,128)(2,1)}, bf16[2,1056,1024]{2,1,0:T(8,128)(2,1)}, bf16[2,512,1024]{2,1,0:T(8,128)(2,1)}, f32[2,1024]{1,0:T(2,128)}) custom-call(bf16[512,1024]{1,0:T(8,128)(2,1)} %get-tuple-element.49.low_own, bf16[512,1024]{1,0:T(8,128)(2,1)} %get-tuple-element.50.low_oth, f32[1,1024]{1,0:T(1,128)} %bitcast.19, ...), custom_call_target="tpu_custom_call" | custom-call | flops 15000000512 | bytes 50000000 | tf_op jit(solution)/shard_map/tail/pallas_call | solution.py:500
  337.8 1.4 fusion
  339.2 4.3 %place_a.1 = (f32[1024,256]{1,0:T(8,128)}, f32[1024,256]{1,0:T(8,128)}, f32[1024,256]{1,0:T(8,128)}, f32[256,1024]{1,0:T(8,128)}) custom-call(bf16[2,512,1024]{2,1,0:T(8,128)(2,1)} %get-tuple-element.63.got), custom_call_target="tpu_custom_call" | custom-call | bytes 6291456 | tf_op jit(solution)/shard_map/place_a/pallas_call | solution.py:92
  343.5 0.0 copy-start
  343.5 6.1 %place_b.1 = (f32[704,1024]{1,0:T(8,128)}, f32[704,1024]{1,0:T(8,128)}, f32[704,1024]{1,0:T(8,128)}) custom-call(bf16[2,1056,1024]{2,1,0:T(8,128)(2,1)} %get-tuple-element.68.got), custom_call_target="tpu_custom_call" | custom-call | bytes 12976128 | tf_op jit(solution)/shard_map/place_b/pallas_call | solution.py:92
  349.6 0.0 copy-start.1
  349.6 0.0 copy-done
  349.6 1.0 copy.27
  350.5 0.6 copy-done.1
  351.2 1.0 copy.28
Async XLA Ops:
  343.5 6.1 %copy-start = (bf16[2,256,1024]{2,1,0:T(8,128)(2,1)S(1)}, bf16[2,256,1024]{2,1,0:T(8,128)(2,1)}, u32[]{:S(2)}) copy-start(bf16[2,256,1024]{2,1,0:T(8,128)(2,1)} %get-tuple-element.86) | copy-start | bytes 3145732
  349.6 1.6 copy-start.1
